TPU v7x, 32 devices: a whole 2x2x4 slice. The times are simulated.
32 devices in a mesh: mom: 2 (over x), pts: 16 (over z, y, core).
Axes of the slice: x: 2, y: 2, z: 4, core: 2. Of those that a mesh axis runs over, the one named last changes fastest.
Arguments:
- amplitudes: bfloat16 [2, 2, 1, 256, 64, 128], P(None, None, None, 'mom'), may hold values from -6 to 6
- val_orbitals: bfloat16 [2, 256, 64, 512], P(None, 'mom'), may hold values from -0.25 to 0.25
- cond_orbitals: bfloat16 [2, 256, 512, 128], P(None, 'mom', 'pts'), may hold values from -0.25 to 0.25
- screened: bfloat16 [2, 256, 512, 512], P(None, None, ('pts', 'mom')), may hold values from -12 to 12
- val_energy: float32 [256, 64], P('mom', 'pts'), may hold values from -2 to -0.5
- cond_energy: float32 [256, 128], P('mom'), may hold values from 0.5 to 2
- grid_of_slot: int32 [256], replicated, may hold values from 0 to 255, as said below
- opposite_slot: int32 [256], P('mom'), may hold values from 0 to 255, as said below
Outputs:
- applied: float32 [2, 2, 1, 256, 64, 128], P(None, None, None, 'mom', 'pts')
Inputs may be any that keep to these rules, and one draw needn't show every extreme that they name: `grid_of_slot`: a permutation of the grid indices. opposite_slot[s] is the slot whose grid index is 255 - grid_of_slot[s]; it is never s, and s and opposite_slot[s] lie in aligned blocks of 128 slots whose first slots differ by 128.
All inputs are finite; a program needn't handle non-finite values.
Results may differ from a plain program's by a relative error of at most 0.006.
Values may be sent and summed in bfloat16 or wider, within the bound.
No kernel may reach another device: no remote copies, remote signals or barrier semaphores. Data moves between devices by JAX's collectives and lax.ppermute only.
A program may use at most 256 MiB of HBM per device.

v0:
```python
import math
import jax
import jax.numpy as jnp
from jax import lax
from jax.sharding import PartitionSpec as P


def partner_2(value, axis, apart):
    mask = 2**apart
    pairs = [(source, source ^ mask) for source in range(lax.axis_size(axis))]
    return lax.ppermute(value, axis, pairs)


def complex_mix(formula, left, right, left_sign, right_sign):
    real_real = jnp.einsum(formula, left[0], right[0], preferred_element_type=jnp.float32)
    imag_imag = jnp.einsum(formula, left[1], right[1], preferred_element_type=jnp.float32)
    real_imag = jnp.einsum(formula, left[0], right[1], preferred_element_type=jnp.float32)
    imag_real = jnp.einsum(formula, left[1], right[0], preferred_element_type=jnp.float32)
    return jnp.stack(
        [
            real_real - left_sign * right_sign * imag_imag,
            right_sign * real_imag + left_sign * imag_real,
        ]
    )


def on_device(
    amplitudes,
    val_orbitals,
    cond_orbitals,
    screened,
    val_energy,
    cond_energy,
    grid_of_slot,
    opposite_slot,
):
    slots_here = opposite_slot.shape[0]
    total_slots = grid_of_slot.shape[0]
    rows_here = val_energy.shape[1]
    frequency = jnp.arange(total_slots, dtype=jnp.int32)
    phases = frequency[:, None] * grid_of_slot[None, :] % total_slots
    angles = phases.astype(jnp.float32) * (2.0 * math.pi / total_slots)
    cosine_table = jnp.cos(angles).astype(jnp.bfloat16)
    sine_table = jnp.sin(angles).astype(jnp.bfloat16)
    half_product = complex_mix("bnkvc,kuc->bnkvu", amplitudes, cond_orbitals, 1.0, 1.0).astype(
        jnp.bfloat16
    )
    pair_values = complex_mix("bnkvu,kvm->bnkum", half_product, val_orbitals, 1.0, -1.0).astype(
        jnp.bfloat16
    )
    flattened = pair_values.reshape(pair_values.shape[:4] + (-1,))
    weights = screened.reshape(2, total_slots, -1)
    inverse_count = 1.0 / total_slots
    whole_k = lax.all_to_all(flattened, "mom", split_axis=4, concat_axis=3, tiled=True)
    spec_real = jnp.einsum(
        "fs,bnsc->bnfc", cosine_table, whole_k[0], preferred_element_type=jnp.float32
    ) + jnp.einsum("fs,bnsc->bnfc", sine_table, whole_k[1], preferred_element_type=jnp.float32)
    spec_imag = jnp.einsum(
        "fs,bnsc->bnfc", cosine_table, whole_k[1], preferred_element_type=jnp.float32
    ) - jnp.einsum("fs,bnsc->bnfc", sine_table, whole_k[0], preferred_element_type=jnp.float32)
    prod_real = (weights[0] * spec_real - weights[1] * spec_imag).astype(jnp.bfloat16)
    prod_imag = (weights[0] * spec_imag + weights[1] * spec_real).astype(jnp.bfloat16)
    back_real = (
        jnp.einsum("fs,bnfc->bnsc", cosine_table, prod_real, preferred_element_type=jnp.float32)
        - jnp.einsum("fs,bnfc->bnsc", sine_table, prod_imag, preferred_element_type=jnp.float32)
    ) * inverse_count
    back_imag = (
        jnp.einsum("fs,bnfc->bnsc", cosine_table, prod_imag, preferred_element_type=jnp.float32)
        + jnp.einsum("fs,bnfc->bnsc", sine_table, prod_real, preferred_element_type=jnp.float32)
    ) * inverse_count
    field_pts = lax.all_to_all(
        jnp.stack([back_real, back_imag]).astype(jnp.bfloat16),
        "mom",
        split_axis=3,
        concat_axis=4,
        tiled=True,
    )
    field_pts = field_pts.reshape(pair_values.shape)
    weighted = complex_mix("bnkum,kvm->bnkvu", field_pts, val_orbitals, 1.0, 1.0).astype(
        jnp.bfloat16
    )
    rows_mine = lax.all_to_all(weighted, "pts", split_axis=4, concat_axis=5, tiled=True)
    band_values = complex_mix(
        "bnkvu,kuc->bnkvc",
        rows_mine,
        lax.all_gather(cond_orbitals, "pts", axis=2, tiled=True),
        1.0,
        -1.0,
    )
    top_bit = lax.axis_size("mom").bit_length() - 2
    partner = partner_2(band_values.astype(jnp.bfloat16), "mom", top_bit).astype(band_values.dtype)
    mirrored = jnp.take(partner, opposite_slot % slots_here, axis=3)
    start_row = lax.axis_index("pts") * rows_here
    own_rows = lax.dynamic_slice_in_dim(amplitudes, start_row, rows_here, 4).astype(jnp.float32)
    energy_gap = cond_energy[:, None, :] - val_energy[:, :, None]
    result_real = energy_gap * own_rows[0, 0] - band_values[0, 0] - mirrored[0, 1]
    result_imag = energy_gap * own_rows[1, 0] - band_values[1, 0] + mirrored[1, 1]
    anti_real = -energy_gap * own_rows[0, 1] + band_values[0, 1] + mirrored[0, 0]
    anti_imag = -energy_gap * own_rows[1, 1] + band_values[1, 1] - mirrored[1, 0]
    return jnp.stack([jnp.stack([result_real, anti_real]), jnp.stack([result_imag, anti_imag])])


def solution(mesh):
    in_specs = (
        P(None, None, None, "mom", None, None),
        P(None, "mom", None, None),
        P(None, "mom", "pts", None),
        P(None, None, ("pts", "mom"), None),
        P("mom", "pts"),
        P("mom", None),
        P(),
        P("mom"),
    )
    out_specs = P(None, None, None, "mom", "pts", None)
    return jax.shard_map(
        on_device, mesh=mesh, in_specs=in_specs, out_specs=out_specs, check_vma=False
    )
```

profile of v0, /device:TPU:0, one launch (start us, length us, event | category | flops | bytes accessed | tf_op | source)
XLA Modules:
  0.0 1007.6 jit_solution(14866260467784046337)
XLA Ops:
  7.3 4.6 fusion.134
  11.9 4.1 fusion.41
  16.0 4.1 fusion.40
  20.1 5.4 fusion.44
  25.5 5.4 fusion.45
  30.9 9.8 fusion.17
  40.7 14.0 %fusion.34 = bf16[2,1,128,32,512]{4,3,0,2,1:T(8,128)(2,1)} fusion(f32[128,2,32,512]{3,2,1,0:T(8,128)} %fusion.17, bf16[2,128,64,32]{2,3,0,1:T(8,128)(2,1)} %fusion.45, bf16[2,128,64,512]{3,2,1,0:T(8,128)(2,1)} %param.9), kind=kOutput, calls=%fused_computation.51 | convolution fusion | flops 549453824 | bytes 35651584 | tf_op jit(solution)/shard_map/bnkvu,kvm->bnkum/dot_general | solution.py:16
  54.7 16.5 %copy.203 = bf16[2,1,128,32,512]{2,0,4,3,1:T(2,128)(2,1)} copy(bf16[2,1,128,32,512]{4,3,0,2,1:T(8,128)(2,1)} %fusion.34) | data formatting | bytes 16777216 | tf_op jit(solution)/shard_map/stack | solution.py:19
  71.2 12.1 %fusion.23 = f32[128,2,32,512]{3,2,1,0:T(8,128)} fusion(bf16[2,128,64,32]{2,3,0,1:T(8,128)(2,1)S(1)} %copy-done.4, bf16[2,128,64,512]{3,2,1,0:T(8,128)(2,1)} %param.9), kind=kOutput, calls=%fused_computation.40 | convolution fusion | flops 536870912 | bytes 26214400 | tf_op jit(solution)/shard_map/bnkvu,kvm->bnkum/dot_general | solution.py:17
  83.4 12.9 %fusion.37 = bf16[2,1,128,32,512]{4,3,0,2,1:T(8,128)(2,1)} fusion(bf16[2,128,64,32]{2,3,0,1:T(8,128)(2,1)S(1)} %copy-done.2, bf16[2,128,64,512]{3,2,1,0:T(8,128)(2,1)} %param.9, f32[128,2,32,512]{3,2,1,0:T(8,128)} %fusion.23), kind=kOutput, calls=%fused_computation.52 | convolution fusion | flops 549453824 | bytes 34603008 | tf_op jit(solution)/shard_map/bnkvu,kvm->bnkum/dot_general | solution.py:18
  96.3 15.7 %copy.204 = bf16[2,1,128,32,512]{2,0,4,3,1:T(2,128)(2,1)} copy(bf16[2,1,128,32,512]{4,3,0,2,1:T(8,128)(2,1)} %fusion.37) | data formatting | bytes 16777216 | tf_op jit(solution)/shard_map/stack | solution.py:19
  112.0 26.4 %pad_maximum_fusion = bf16[2,2,1,128,16384]{3,1,2,0,4:T(2,128)(2,1)} fusion(bf16[1,2,1,128,16384]{3,1,2,0,4:T(2,128)(2,1)} %bitcast.316, bf16[1,2,1,128,16384]{3,1,2,0,4:T(2,128)(2,1)} %bitcast.315), kind=kLoop, calls=%fused_computation.3 | loop fusion | flops 8388608 | bytes 33554432 | tf_op jit(solution)/shard_map/stack | solution.py:19
  138.4 9.8 all-to-all-start
  148.2 12.1 %slice_convert_fusion.1 = (f32[1,256,16,512]{3,2,1,0:T(8,128)}, f32[1,256,16,512]{3,2,1,0:T(8,128)}) fusion(bf16[2,256,16,512]{3,2,1,0:T(8,128)(2,1)} %param.11), kind=kLoop, calls=%fused_computation.61 | loop fusion | flops 4194304 | bytes 25165824 | tf_op jit(solution)/shard_map/convert_element_type | solution.py:61
  160.3 9.9 copy.202
  170.2 10.0 copy.205
  180.2 150.9 %all-to-all-done = bf16[2,2,1,128,16384]{3,1,2,0,4:T(2,128)(2,1)} async-done(((bf16[2,2,1,128,16384]{3,1,2,0,4:T(2,128)(2,1)}), bf16[2,2,1,128,16384]{3,1,2,0,4:T(2,128)(2,1)}, u32[]{:S(2)}, u32[]{:S(2)}) %all-to-all-start) | async-done | bytes 16777248 | tf_op jit(solution)/shard_map/all_to_all | solution.py:54
  331.1 28.1 %copy.246 = bf16[2,2,1,128,2,8192]{3,4,5,1,2,0:T(2,128)(2,1)S(1)} copy(bf16[2,2,1,128,2,8192]{3,1,0,5,4,2:T(2,128)(2,1)} %bitcast.38) | data formatting | bytes 33554432 | tf_op jit(solution)/shard_map/all_to_all | solution.py:54
  359.2 13.0 %fusion.133 = (bf16[1,2,1,2,128,8192]{4,3,5,1,2,0:T(2,128)(2,1)}, bf16[1,2,1,2,128,8192]{4,3,5,1,2,0:T(2,128)(2,1)}) fusion(bf16[2,2,1,2,128,8192]{4,3,5,1,2,0:T(2,128)(2,1)S(1)} %bitcast.312), kind=kLoop, calls=%fused_computation.179 | loop fusion | bytes 33554432 | tf_op jit(solution)/shard_map/slice | solution.py:57
  372.2 14.1 %reshape.539 = bf16[2,256,8192]{1,2,0:T(8,128)(2,1)} reshape(bf16[1,2,1,2,128,8192]{4,3,5,1,2,0:T(2,128)(2,1)} %get-tuple-element.15) | data formatting | bytes 16777216 | tf_op jit(solution)/shard_map/reshape.28
  386.3 14.2 %reshape.538 = bf16[2,256,8192]{1,2,0:T(8,128)(2,1)} reshape(bf16[1,2,1,2,128,8192]{4,3,5,1,2,0:T(2,128)(2,1)} %get-tuple-element.16) | data formatting | bytes 16777216 | tf_op jit(solution)/shard_map/reshape.24
  400.5 12.5 %fusion.91 = f32[2,8192,256]{2,1,0:T(8,128)} fusion(bf16[2,256,8192]{1,2,0:T(8,128)(2,1)} %reshape.539, s32[256]{0:T(256)S(1)} %copy-done.6), kind=kOutput, calls=%fused_computation.134 | convolution fusion | flops 2148466688 | bytes 25166848 | tf_op jit(solution)/shard_map/fs,bnsc->bnfc/dot_general | solution.py:58
  413.1 9.0 fusion.93
  422.1 14.8 %convolution_subtract_fusion = f32[2,8192,256]{2,1,0:T(8,128)} fusion(f32[2,8192,256]{2,1,0:T(8,128)} %fusion.91, bf16[2,256,8192]{1,2,0:T(8,128)(2,1)S(1)} %copy-done.1, s32[256]{0:T(256)S(1)} %copy-done.6), kind=kOutput, calls=%fused_computation.23 | convolution fusion | flops 2152660992 | bytes 41944064 | tf_op jit(solution)/shard_map/fs,bnsc->bnfc/dot_general | solution.py:60
  436.9 27.2 %fusion.11 = (bf16[2,256,8192]{1,2,0:T(8,128)(2,1)}, bf16[2,256,8192]{1,2,0:T(8,128)(2,1)}) fusion(f32[2,8192,256]{2,1,0:T(8,128)} %convolution_subtract_fusion, f32[256,8192]{0,1:T(8,128)} %bitcast.311, f32[256,8192]{0,1:T(8,128)} %bitcast.310, f32[2,8192,256]{2,1,0:T(8,128)} %fusion.93, bf16[2,256,8192]{1,2,0:T(8,128)(2,1)} %reshape.539, s32[256]{0:T(256)S(1)} %copy-done.6), kind=kOutput, calls=%fused_computation.28 | convolution fusion | flops 2186215424 | bytes 75498496 | tf_op jit(solution)/shard_map/fs,bnsc->bnfc/dot_general | solution.py:57
  464.1 12.5 %fusion.89 = f32[2,8192,256]{2,1,0:T(8,128)} fusion(bf16[2,256,8192]{1,2,0:T(8,128)(2,1)} %get-tuple-element.11, s32[256]{0:T(256)S(1)} %copy-done.6), kind=kOutput, calls=%fused_computation.133 | convolution fusion | flops 2148466688 | bytes 25166848 | tf_op jit(solution)/shard_map/fs,bnfc->bnsc/dot_general | solution.py:64
  476.7 9.0 fusion.87
  485.7 13.5 %fusion.8 = bf16[1,2,1,256,8192]{3,4,1,2,0:T(8,128)(2,1)} fusion(f32[2,8192,256]{2,1,0:T(8,128)} %fusion.89, bf16[2,256,8192]{1,2,0:T(8,128)(2,1)} %get-tuple-element.12, s32[256]{0:T(256)S(1)} %copy-done.6), kind=kOutput, calls=%fused_computation.25 | convolution fusion | flops 2161049600 | bytes 33555456 | tf_op jit(solution)/shard_map/fs,bnfc->bnsc/dot_general | solution.py:65
  499.2 11.5 %fusion.9 = bf16[1,2,1,256,8192]{3,4,1,2,0:T(8,128)(2,1)} fusion(f32[2,8192,256]{2,1,0:T(8,128)} %fusion.87, bf16[2,256,8192]{1,2,0:T(8,128)(2,1)S(1)} %bitcast.309, s32[256]{0:T(256)S(1)} %copy-done.6), kind=kOutput, calls=%fused_computation.26 | convolution fusion | flops 2161049600 | bytes 33555456 | tf_op jit(solution)/shard_map/fs,bnfc->bnsc/dot_general | solution.py:69
  510.8 13.7 %pad_maximum_fusion.1 = bf16[2,2,1,256,8192]{3,4,1,2,0:T(8,128)(2,1)} fusion(bf16[1,2,1,256,8192]{3,4,1,2,0:T(8,128)(2,1)} %fusion.9, bf16[1,2,1,256,8192]{3,4,1,2,0:T(8,128)(2,1)} %fusion.8), kind=kLoop, calls=%fused_computation.4 | loop fusion | flops 8388608 | bytes 33554432 | tf_op jit(solution)/shard_map/stack | solution.py:72
  524.5 41.2 %copy.175 = bf16[2,2,1,256,8192]{4,1,2,0,3:T(2,128)(2,1)} copy(bf16[2,2,1,256,8192]{3,4,1,2,0:T(8,128)(2,1)} %pad_maximum_fusion.1) | data formatting | bytes 33554432 | tf_op jit(solution)/shard_map/stack | solution.py:72
  565.7 200.1 %all_to_all.45 = bf16[2,2,1,256,8192]{4,1,2,0,3:T(2,128)(2,1)} all-to-all(bf16[2,2,1,256,8192]{4,1,2,0,3:T(2,128)(2,1)} %copy.175), channel_id=1, replica_groups=mesh['mom'=2,'pts'=16] {'mom'}, dimensions={3} | all-to-all | bytes 33554432 | tf_op jit(solution)/shard_map/all_to_all | solution.py:71
  765.8 30.2 %copy.245 = bf16[2,2,1,2,128,8192]{5,3,1,4,2,0:T(2,128)(2,1)S(1)} copy(bf16[2,2,1,2,128,8192]{5,1,0,4,3,2:T(2,128)(2,1)} %bitcast.314) | data formatting | bytes 33554432 | tf_op jit(solution)/shard_map/all_to_all | solution.py:71
  796.1 14.9 %fusion.132 = (bf16[1,2,1,128,2,8192]{5,4,1,3,2,0:T(2,128)(2,1)}, bf16[1,2,1,128,2,8192]{5,4,1,3,2,0:T(2,128)(2,1)}) fusion(bf16[2,2,1,128,2,8192]{5,4,1,3,2,0:T(2,128)(2,1)S(1)} %bitcast.313), kind=kLoop, calls=%fused_computation.178 | loop fusion | bytes 33554432 | tf_op jit(solution)/shard_map/slice | solution.py:15
  811.0 14.3 %reshape.542 = bf16[2,128,32,512]{3,2,0,1:T(8,128)(2,1)} reshape(bf16[1,2,1,128,2,8192]{5,4,1,3,2,0:T(2,128)(2,1)} %get-tuple-element.13) | data formatting | bytes 16777216 | tf_op jit(solution)/shard_map/reshape.50
  825.2 14.3 %reshape.543 = bf16[2,128,32,512]{3,2,0,1:T(8,128)(2,1)} reshape(bf16[1,2,1,128,2,8192]{5,4,1,3,2,0:T(2,128)(2,1)} %get-tuple-element.14) | data formatting | bytes 16777216 | tf_op jit(solution)/shard_map/reshape.54
  839.5 10.1 fusion.14
  849.6 10.1 fusion.12
  859.6 9.3 fusion.46
  868.9 10.7 %fusion.47 = bf16[1,2,1,128,64,32]{4,5,1,3,2,0:T(8,128)(2,1)} fusion(f32[128,2,32,64]{3,2,1,0:T(8,128)} %fusion.12, bf16[2,128,32,512]{3,2,0,1:T(8,128)(2,1)} %reshape.542, bf16[2,128,64,512]{3,2,1,0:T(8,128)(2,1)} %param.9), kind=kOutput, calls=%fused_computation.69 | convolution fusion | flops 537919488 | bytes 22020096 | tf_op jit(solution)/shard_map/bnkum,kvm->bnkvu/dot_general | solution.py:17
  879.6 4.6 pad_maximum_fusion.2
  884.2 8.0 copy.177
  892.1 52.0 %all_to_all.46 = bf16[2,2,1,128,64,32]{3,5,2,1,0,4:T(8,128)(2,1)S(1)} all-to-all(bf16[2,2,1,128,64,32]{3,5,2,1,0,4:T(8,128)(2,1)S(1)} %copy.177), channel_id=1, replica_groups=mesh['mom'=2,'pts'=16] {'pts'}, dimensions={4} | all-to-all | bytes 4194304 | tf_op jit(solution)/shard_map/all_to_all | solution.py:82
  949.2 7.0 fusion.5
  956.3 7.1 fusion.6
  963.3 7.0 fusion.4
  970.4 7.1 fusion.7
  980.9 12.8 %collective-permute-done = bf16[2,2,1,128,4,128]{5,3,4,2,1,0:T(8,128)(2,1)S(1)} collective-permute-done((bf16[2,2,1,128,4,128]{5,3,4,2,1,0:T(8,128)(2,1)S(1)}, bf16[2,2,1,128,4,128]{5,3,4,2,1,0:T(8,128)(2,1)S(1)}, u32[]{:S(2)}, u32[]{:S(2)}) %collective-permute-start) | collective-permute-done | bytes 524320 | tf_op jit(solution)/shard_map/ppermute | solution.py:11
  (58 shorter events, 16.0 us)
Async XLA Ops:
  6.5 942.7 %all-gather.2.cloned.1.call-start = ((), (), s32[]{:S(2)}) async-start(), calls=%async_computation.3 | async-start | bytes 35651584 | tf_op jit(solution)/shard_map/all_gather | solution.py:86
  7.3 4.6 copy-start.3
  16.0 14.9 %slice-start = ((s8[16777216]{0:T(1024)(128)(4,1)}), s8[4194304]{0:T(1024)(128)(4,1)S(1)}, s32[]{:S(2)}) async-start(s8[16777216]{0:T(1024)(128)(4,1)} %bitcast.306), calls=%async_computation.4 | async-start | bytes 8388608
  16.0 14.9 %slice-start.1 = ((s8[16777216]{0:T(1024)(128)(4,1)}), s8[4194304]{0:T(1024)(128)(4,1)S(1)}, s32[]{:S(2)}) async-start(s8[16777216]{0:T(1024)(128)(4,1)} %bitcast.306), calls=%async_computation.5 | async-start | bytes 8388608
  20.0 10.8 %slice-start.2 = ((s8[16777216]{0:T(1024)(128)(4,1)}), s8[4194304]{0:T(1024)(128)(4,1)S(1)}, s32[]{:S(2)}) async-start(s8[16777216]{0:T(1024)(128)(4,1)} %bitcast.306), calls=%async_computation.6 | async-start | bytes 8388608
  25.5 5.4 slice-start.3
  54.7 16.5 %copy-start.4 = (bf16[2,128,64,32]{2,3,0,1:T(8,128)(2,1)S(1)}, bf16[2,128,64,32]{2,3,0,1:T(8,128)(2,1)}, u32[]{:S(2)}) copy-start(bf16[2,128,64,32]{2,3,0,1:T(8,128)(2,1)} %fusion.44) | copy-start | bytes 3145732
  71.2 12.1 %copy-start.2 = (bf16[2,128,64,32]{2,3,0,1:T(8,128)(2,1)S(1)}, bf16[2,128,64,32]{2,3,0,1:T(8,128)(2,1)}, u32[]{:S(2)}) copy-start(bf16[2,128,64,32]{2,3,0,1:T(8,128)(2,1)} %fusion.45) | copy-start | bytes 3145732
  138.4 192.7 %all-to-all-start = ((bf16[2,2,1,128,16384]{3,1,2,0,4:T(2,128)(2,1)}), bf16[2,2,1,128,16384]{3,1,2,0,4:T(2,128)(2,1)}, u32[]{:S(2)}, u32[]{:S(2)}) async-start(bf16[2,2,1,128,16384]{3,1,2,0,4:T(2,128)(2,1)} %pad_maximum_fusion), calls=%async_computation | async-start | bytes 33554432 | tf_op jit(solution)/shard_map/all_to_all | solution.py:54
  386.3 14.2 %copy-start.6 = (s32[256]{0:T(256)S(1)}, s32[256]{0:T(256)}, u32[]{:S(2)}) copy-start(s32[256]{0:T(256)} %param.14) | copy-start | bytes 3076
  400.5 12.6 %copy-start.1 = (bf16[2,256,8192]{1,2,0:T(8,128)(2,1)S(1)}, bf16[2,256,8192]{1,2,0:T(8,128)(2,1)}, u32[]{:S(2)}) copy-start(bf16[2,256,8192]{1,2,0:T(8,128)(2,1)} %reshape.538) | copy-start | bytes 25165828
  464.1 12.6 %copy-start = (bf16[2,256,8192]{1,2,0:T(8,128)(2,1)S(1)}, bf16[2,256,8192]{1,2,0:T(8,128)(2,1)}, u32[]{:S(2)}) copy-start(bf16[2,256,8192]{1,2,0:T(8,128)(2,1)} %get-tuple-element.12) | copy-start | bytes 25165828
  464.1 35.1 %slice-start.4 = ((s8[8388608]{0:T(1024)(128)(4,1)}), s8[4194304]{0:T(1024)(128)(4,1)S(1)}, s32[]{:S(2)}) async-start(s8[8388608]{0:T(1024)(128)(4,1)} %bitcast.308), calls=%async_computation.8 | async-start | bytes 8388608
  476.7 22.5 %slice-start.5 = ((s8[8388608]{0:T(1024)(128)(4,1)}), s8[4194304]{0:T(1024)(128)(4,1)S(1)}, s32[]{:S(2)}) async-start(s8[8388608]{0:T(1024)(128)(4,1)} %bitcast.308), calls=%async_computation.9 | async-start | bytes 8388608
  970.4 8.9 copy-start.8
  977.5 18.9 %copy-start.5 = (f32[128,128]{1,0:T(8,128)S(1)}, f32[128,128]{1,0:T(8,128)}, u32[]{:S(2)}) copy-start(f32[128,128]{1,0:T(8,128)} %param.13) | copy-start | bytes 196612
  977.5 18.9 %copy-start.7 = (f32[128,4]{0,1:T(4,128)S(1)}, f32[128,4]{0,1:T(4,128)}, u32[]{:S(2)}) copy-start(f32[128,4]{0,1:T(4,128)} %param.12) | copy-start | bytes 6148
  978.9 14.9 %collective-permute-start = (bf16[2,2,1,128,4,128]{5,3,4,2,1,0:T(8,128)(2,1)S(1)}, bf16[2,2,1,128,4,128]{5,3,4,2,1,0:T(8,128)(2,1)S(1)}, u32[]{:S(2)}, u32[]{:S(2)}) collective-permute-start(bf16[2,2,1,128,4,128]{5,3,4,2,1,0:T(8,128)(2,1)S(1)} %pad_maximum_fusion.4), channel_id=1, source_target_pairs={{0,16},{16,0},{1,17},{17,1},{2,18},{18,2},{3,19},{19,3},{4,20},{20... | collective-permute-start | bytes 1572872 | tf_op jit(solution)/shard_map/ppermute | solution.py:11
Sparse Core Ops, SparseCore 0:
  8.9 170.7 all-gather.1
where the time goes:
time: 1020 us; the launch traced here: 1010 us
  local copies, waits for them, and re-layouts  259 us (25%)
  blocking collectives  252 us (25%)
  matrix products  246 us (24%)
  waiting for transfers between devices  164 us (16%)
  other arithmetic  61.5 us (6%)
  between operations  13.9 us (1%)
    all_to_all x1, blocking collectives, on_device(): lax.all_to_all(jnp.stack([back_real, back_imag]).astype(jnp.bfloat16), 'm...  200 us
    all_to_all x1, waiting for transfers between devices, on_device(): lax.all_to_all(flattened, 'mom', split_axis=4, concat_axis=3, tiled=True)  151 us
    another operation x6, local copies, waits for them, and re-layouts  58.6 us
    all_to_all x1, blocking collectives, on_device(): lax.all_to_all(weighted, 'pts', split_axis=4, concat_axis=5, tiled=True)  52 us
    another operation x1, local copies, waits for them, and re-layouts, on_device(): jnp.stack([back_real, back_imag]).astype(jnp.bfloat16)  41.2 us
    another operation x3, local copies, waits for them, and re-layouts, complex_mix(): jnp.stack([real_real - left_sign * right_sign * imag_imag, right_sign * r...  40.2 us
    dot_general x4, matrix products, complex_mix(): jnp.einsum(formula, left[1], right[1], preferred_element_type=jnp.float32)  35.8 us
    dot_general x4, matrix products, complex_mix(): jnp.einsum(formula, left[1], right[0], preferred_element_type=jnp.float32)  35.4 us
  transfers between devices with their start and end apart: 3, of which 2 were waited for; matrix products, arithmetic and copies ran while one was open for 53% of the time, Pallas kernels for 0%

commit v1 on v0

--- a/solution.py
+++ b/solution.py
@@ -3,6 +3,30 @@
 import jax.numpy as jnp
 from jax import lax
 from jax.sharding import PartitionSpec as P
+
+
+def split_up(shard, dim, count):
+    shape = shard.shape
+    parts = shard.reshape(*shape[:dim], count, shape[dim] // count, *shape[dim + 1 :])
+    return jnp.moveaxis(parts, dim, 0)
+
+
+def in_order(parts, dim):
+    parts = jnp.moveaxis(parts, 0, dim)
+    dims = parts.shape
+    return parts.reshape(*dims[:dim], dims[dim] * dims[dim + 1], *dims[dim + 2 :])
+
+
+def sent_to_each(array, axis, split_dim, concat_dim):
+    length, index = (lax.axis_size(axis), lax.axis_index(axis))
+    blocks = split_up(array, split_dim, length)
+    out = blocks
+    for step in range(1, length):
+        target, source = ((index + step) % length, (index - step) % length)
+        sent = lax.dynamic_index_in_dim(blocks, target, 0)
+        received = lax.ppermute(sent, axis, [(i, (i + step) % length) for i in range(length)])
+        out = lax.dynamic_update_slice_in_dim(out, received, source, axis=0)
+    return in_order(out, concat_dim)
 
 
 def partner_2(value, axis, apart):
@@ -79,7 +103,7 @@
     weighted = complex_mix("bnkum,kvm->bnkvu", field_pts, val_orbitals, 1.0, 1.0).astype(
         jnp.bfloat16
     )
-    rows_mine = lax.all_to_all(weighted, "pts", split_axis=4, concat_axis=5, tiled=True)
+    rows_mine = sent_to_each(weighted, "pts", 4, 5)
     band_values = complex_mix(
         "bnkvu,kuc->bnkvc",
         rows_mine,

time: 1020 us -> 1010 us (level)
  blocking collectives: 252 us -> 0 us
  waiting for transfers between devices: 164 us -> 370 us
  starting transfers between devices: 10.2 us -> 48.9 us
    all_to_all x2 -> x0, blocking collectives: 252 us -> none  [the longest x1 200 us: on_device(): lax.all_to_all(jnp.stack([back_real, back_imag]).astype(jnp.bfloat16), 'm...]
    all_to_all x0 -> x1, waiting for transfers between devices: none -> 181 us  [on_device(): lax.all_to_all(jnp.stack([back_real, back_imag]).astype(jnp.bfloat16), 'm...]
    ppermute x0 -> x15, starting transfers between devices: none -> 28.7 us  [sent_to_each(): lax.ppermute(sent, axis, [(i, (i + step) % length) for i in range(length)])]
    ppermute x0 -> x15, waiting for transfers between devices: none -> 25.2 us  [sent_to_each(): lax.ppermute(sent, axis, [(i, (i + step) % length) for i in range(length)])]
    another operation x3 -> x2, local copies, waits for them, and re-layouts: 40.2 us -> 32.2 us  [complex_mix(): jnp.stack([real_real - left_sign * right_sign * imag_imag, right_sign * r...]
    another operation x3 -> x2, other arithmetic: 31.1 us -> 26.5 us  [complex_mix(): jnp.stack([real_real - left_sign * right_sign * imag_imag, right_sign * r...]
  transfers between devices with their start and end apart: 3 -> 19, of which waited for: 2 -> 9; matrix products, arithmetic and copies ran while one was open for 53% -> 53% of each run, Pallas kernels for 0% -> 0%
where the time goes in v1:
time: 1010 us; the launch traced here: 997 us
  waiting for transfers between devices  370 us (37%)
  local copies, waits for them, and re-layouts  259 us (26%)
  matrix products  247 us (24%)
  other arithmetic  57.4 us (6%)
  starting transfers between devices  48.9 us (5%)
  between operations  14.7 us (1%)
    all_to_all x1, waiting for transfers between devices, on_device(): lax.all_to_all(jnp.stack([back_real, back_imag]).astype(jnp.bfloat16), 'm...  181 us
    all_to_all x1, waiting for transfers between devices, on_device(): lax.all_to_all(flattened, 'mom', split_axis=4, concat_axis=3, tiled=True)  151 us
    another operation x6, local copies, waits for them, and re-layouts  58.8 us
    another operation x1, local copies, waits for them, and re-layouts, on_device(): jnp.stack([back_real, back_imag]).astype(jnp.bfloat16)  41.2 us
    dot_general x4, matrix products, complex_mix(): jnp.einsum(formula, left[1], right[1], preferred_element_type=jnp.float32)  35.8 us
    dot_general x4, matrix products, complex_mix(): jnp.einsum(formula, left[1], right[0], preferred_element_type=jnp.float32)  35.6 us
    dot_general x4, matrix products, complex_mix(): jnp.einsum(formula, left[0], right[1], preferred_element_type=jnp.float32)  33.9 us
    another operation x2, local copies, waits for them, and re-layouts, complex_mix(): jnp.stack([real_real - left_sign * right_sign * imag_imag, right_sign * r...  32.2 us
  transfers between devices with their start and end apart: 19, of which 9 were waited for; matrix products, arithmetic and copies ran while one was open for 53% of the time, Pallas kernels for 0%

profile of v1, /device:TPU:0, one launch (start us, length us, event | category | flops | bytes accessed | tf_op | source)
XLA Modules:
  0.0 997.3 jit_solution(3504902925507853412)
XLA Ops:
  7.3 4.6 fusion.165
  20.1 5.4 fusion.44
  25.5 5.4 fusion.45
  30.9 9.8 fusion.17
  40.8 14.0 %fusion.34 = bf16[2,1,128,32,512]{4,3,0,2,1:T(8,128)(2,1)} fusion(f32[128,2,32,512]{3,2,1,0:T(8,128)} %fusion.17, bf16[2,128,64,32]{2,3,0,1:T(8,128)(2,1)} %fusion.45, bf16[2,128,64,512]{3,2,1,0:T(8,128)(2,1)} %param.9), kind=kOutput, calls=%fused_computation.82 | convolution fusion | flops 549453824 | bytes 35651584 | tf_op jit(solution)/shard_map/bnkvu,kvm->bnkum/dot_general | solution.py:40
  54.8 16.5 %copy.204 = bf16[2,1,128,32,512]{2,0,4,3,1:T(2,128)(2,1)} copy(bf16[2,1,128,32,512]{4,3,0,2,1:T(8,128)(2,1)} %fusion.34) | data formatting | bytes 16777216 | tf_op jit(solution)/shard_map/stack | solution.py:43
  71.3 12.1 %fusion.23 = f32[128,2,32,512]{3,2,1,0:T(8,128)} fusion(bf16[2,128,64,32]{2,3,0,1:T(8,128)(2,1)S(1)} %copy-done.4, bf16[2,128,64,512]{3,2,1,0:T(8,128)(2,1)} %param.9), kind=kOutput, calls=%fused_computation.40 | convolution fusion | flops 536870912 | bytes 26214400 | tf_op jit(solution)/shard_map/bnkvu,kvm->bnkum/dot_general | solution.py:41
  83.4 12.9 %fusion.37 = bf16[2,1,128,32,512]{4,3,0,2,1:T(8,128)(2,1)} fusion(bf16[2,128,64,32]{2,3,0,1:T(8,128)(2,1)S(1)} %copy-done.2, bf16[2,128,64,512]{3,2,1,0:T(8,128)(2,1)} %param.9, f32[128,2,32,512]{3,2,1,0:T(8,128)} %fusion.23), kind=kOutput, calls=%fused_computation.83 | convolution fusion | flops 549453824 | bytes 34603008 | tf_op jit(solution)/shard_map/bnkvu,kvm->bnkum/dot_general | solution.py:42
  96.3 15.7 %copy.205 = bf16[2,1,128,32,512]{2,0,4,3,1:T(2,128)(2,1)} copy(bf16[2,1,128,32,512]{4,3,0,2,1:T(8,128)(2,1)} %fusion.37) | data formatting | bytes 16777216 | tf_op jit(solution)/shard_map/stack | solution.py:43
  112.0 26.4 %pad_maximum_fusion = bf16[2,2,1,128,16384]{3,1,2,0,4:T(2,128)(2,1)} fusion(bf16[1,2,1,128,16384]{3,1,2,0,4:T(2,128)(2,1)} %bitcast.343, bf16[1,2,1,128,16384]{3,1,2,0,4:T(2,128)(2,1)} %bitcast.342), kind=kLoop, calls=%fused_computation.3 | loop fusion | flops 8388608 | bytes 33554432 | tf_op jit(solution)/shard_map/stack | solution.py:43
  138.4 9.8 all-to-all-start
  148.3 12.1 %slice_convert_fusion.1 = (f32[1,256,16,512]{3,2,1,0:T(8,128)}, f32[1,256,16,512]{3,2,1,0:T(8,128)}) fusion(bf16[2,256,16,512]{3,2,1,0:T(8,128)(2,1)} %param.11), kind=kLoop, calls=%fused_computation.91 | loop fusion | flops 4194304 | bytes 25165824 | tf_op jit(solution)/shard_map/convert_element_type | solution.py:85
  160.4 9.9 copy.203
  170.3 10.1 %copy.206 = f32[1,256,16,512]{1,3,2,0:T(8,128)} copy(f32[1,256,16,512]{3,2,1,0:T(8,128)} %get-tuple-element.18) | data formatting | bytes 16777216 | tf_op jit(solution)/shard_map/convert_element_type | solution.py:85
  180.4 150.8 %all-to-all-done = bf16[2,2,1,128,16384]{3,1,2,0,4:T(2,128)(2,1)} async-done(((bf16[2,2,1,128,16384]{3,1,2,0,4:T(2,128)(2,1)}), bf16[2,2,1,128,16384]{3,1,2,0,4:T(2,128)(2,1)}, u32[]{:S(2)}, u32[]{:S(2)}) %all-to-all-start) | async-done | bytes 16777248 | tf_op jit(solution)/shard_map/all_to_all | solution.py:78
  331.2 28.1 %copy.247 = bf16[2,2,1,128,2,8192]{3,4,5,1,2,0:T(2,128)(2,1)S(1)} copy(bf16[2,2,1,128,2,8192]{3,1,0,5,4,2:T(2,128)(2,1)} %bitcast.38) | data formatting | bytes 33554432 | tf_op jit(solution)/shard_map/all_to_all | solution.py:78
  359.2 13.0 %fusion.164 = (bf16[1,2,1,2,128,8192]{4,3,5,1,2,0:T(2,128)(2,1)}, bf16[1,2,1,2,128,8192]{4,3,5,1,2,0:T(2,128)(2,1)}) fusion(bf16[2,2,1,2,128,8192]{4,3,5,1,2,0:T(2,128)(2,1)S(1)} %bitcast.340), kind=kLoop, calls=%fused_computation.255 | loop fusion | bytes 33554432 | tf_op jit(solution)/shard_map/slice | solution.py:81
  372.3 14.1 %reshape.560 = bf16[2,256,8192]{1,2,0:T(8,128)(2,1)} reshape(bf16[1,2,1,2,128,8192]{4,3,5,1,2,0:T(2,128)(2,1)} %get-tuple-element.15) | data formatting | bytes 16777216 | tf_op jit(solution)/shard_map/reshape.30
  386.3 14.2 %reshape.559 = bf16[2,256,8192]{1,2,0:T(8,128)(2,1)} reshape(bf16[1,2,1,2,128,8192]{4,3,5,1,2,0:T(2,128)(2,1)} %get-tuple-element.16) | data formatting | bytes 16777216 | tf_op jit(solution)/shard_map/reshape.26
  400.6 12.6 %fusion.107 = f32[2,8192,256]{2,1,0:T(8,128)} fusion(bf16[2,256,8192]{1,2,0:T(8,128)(2,1)} %reshape.560, s32[256]{0:T(256)S(1)} %copy-done.6), kind=kOutput, calls=%fused_computation.180 | convolution fusion | flops 2148466688 | bytes 25166848 | tf_op jit(solution)/shard_map/fs,bnsc->bnfc/dot_general | solution.py:82
  413.1 9.1 fusion.109
  422.2 14.8 %convolution_subtract_fusion = f32[2,8192,256]{2,1,0:T(8,128)} fusion(f32[2,8192,256]{2,1,0:T(8,128)} %fusion.107, bf16[2,256,8192]{1,2,0:T(8,128)(2,1)S(1)} %copy-done.1, s32[256]{0:T(256)S(1)} %copy-done.6), kind=kOutput, calls=%fused_computation.23 | convolution fusion | flops 2152660992 | bytes 41944064 | tf_op jit(solution)/shard_map/fs,bnsc->bnfc/dot_general | solution.py:84
  437.0 27.2 %fusion.11 = (bf16[2,256,8192]{1,2,0:T(8,128)(2,1)}, bf16[2,256,8192]{1,2,0:T(8,128)(2,1)}) fusion(f32[2,8192,256]{2,1,0:T(8,128)} %convolution_subtract_fusion, f32[256,8192]{0,1:T(8,128)} %bitcast.339, f32[256,8192]{0,1:T(8,128)} %bitcast.338, f32[2,8192,256]{2,1,0:T(8,128)} %fusion.109, bf16[2,256,8192]{1,2,0:T(8,128)(2,1)} %reshape.560, ...), kind=kOutput, calls=%fused_computation.28 | convolution fusion | flops 2186215424 | bytes 75498496 | tf_op jit(solution)/shard_map/fs,bnsc->bnfc/dot_general | solution.py:81
  464.2 12.6 %fusion.105 = f32[2,8192,256]{2,1,0:T(8,128)} fusion(bf16[2,256,8192]{1,2,0:T(8,128)(2,1)} %get-tuple-element.11, s32[256]{0:T(256)S(1)} %copy-done.6), kind=kOutput, calls=%fused_computation.179 | convolution fusion | flops 2148466688 | bytes 25166848 | tf_op jit(solution)/shard_map/fs,bnfc->bnsc/dot_general | solution.py:88
  476.8 9.0 fusion.103
  485.8 13.7 %fusion.8 = bf16[1,2,1,256,8192]{3,4,1,2,0:T(8,128)(2,1)} fusion(f32[2,8192,256]{2,1,0:T(8,128)} %fusion.105, bf16[2,256,8192]{1,2,0:T(8,128)(2,1)} %get-tuple-element.12, s32[256]{0:T(256)S(1)} %copy-done.6), kind=kOutput, calls=%fused_computation.25 | convolution fusion | flops 2161049600 | bytes 33555456 | tf_op jit(solution)/shard_map/fs,bnfc->bnsc/dot_general | solution.py:89
  499.5 11.4 %fusion.9 = bf16[1,2,1,256,8192]{3,4,1,2,0:T(8,128)(2,1)} fusion(f32[2,8192,256]{2,1,0:T(8,128)} %fusion.103, bf16[2,256,8192]{1,2,0:T(8,128)(2,1)S(1)} %bitcast.337, s32[256]{0:T(256)S(1)} %copy-done.6), kind=kOutput, calls=%fused_computation.26 | convolution fusion | flops 2161049600 | bytes 33555456 | tf_op jit(solution)/shard_map/fs,bnfc->bnsc/dot_general | solution.py:93
  511.0 13.8 %pad_maximum_fusion.1 = bf16[2,2,1,256,8192]{3,4,1,2,0:T(8,128)(2,1)} fusion(bf16[1,2,1,256,8192]{3,4,1,2,0:T(8,128)(2,1)} %fusion.9, bf16[1,2,1,256,8192]{3,4,1,2,0:T(8,128)(2,1)} %fusion.8), kind=kLoop, calls=%fused_computation.4 | loop fusion | flops 8388608 | bytes 33554432 | tf_op jit(solution)/shard_map/stack | solution.py:96
  524.8 41.2 %copy.176 = bf16[2,2,1,256,8192]{4,1,2,0,3:T(2,128)(2,1)} copy(bf16[2,2,1,256,8192]{3,4,1,2,0:T(8,128)(2,1)} %pad_maximum_fusion.1) | data formatting | bytes 33554432 | tf_op jit(solution)/shard_map/stack | solution.py:96
  565.9 9.7 all-to-all-start.1
  576.2 181.5 %all-to-all-done.1 = bf16[2,2,1,256,8192]{4,1,2,0,3:T(2,128)(2,1)} async-done(((bf16[2,2,1,256,8192]{4,1,2,0,3:T(2,128)(2,1)}), bf16[2,2,1,256,8192]{4,1,2,0,3:T(2,128)(2,1)}, u32[]{:S(2)}, u32[]{:S(2)}) %all-to-all-start.1) | async-done | bytes 16777248 | tf_op jit(solution)/shard_map/all_to_all | solution.py:95
  757.7 30.2 %copy.246 = bf16[2,2,1,2,128,8192]{5,3,1,4,2,0:T(2,128)(2,1)S(1)} copy(bf16[2,2,1,2,128,8192]{5,1,0,4,3,2:T(2,128)(2,1)} %bitcast.57) | data formatting | bytes 33554432 | tf_op jit(solution)/shard_map/all_to_all | solution.py:95
  787.9 14.9 %fusion.163 = (bf16[1,2,1,128,2,8192]{5,4,1,3,2,0:T(2,128)(2,1)}, bf16[1,2,1,128,2,8192]{5,4,1,3,2,0:T(2,128)(2,1)}) fusion(bf16[2,2,1,128,2,8192]{5,4,1,3,2,0:T(2,128)(2,1)S(1)} %bitcast.341), kind=kLoop, calls=%fused_computation.254 | loop fusion | bytes 33554432 | tf_op jit(solution)/shard_map/slice | solution.py:39
  802.8 14.3 %reshape.563 = bf16[2,128,32,512]{3,2,0,1:T(8,128)(2,1)} reshape(bf16[1,2,1,128,2,8192]{5,4,1,3,2,0:T(2,128)(2,1)} %get-tuple-element.13) | data formatting | bytes 16777216 | tf_op jit(solution)/shard_map/reshape.52
  817.1 14.3 %reshape.564 = bf16[2,128,32,512]{3,2,0,1:T(8,128)(2,1)} reshape(bf16[1,2,1,128,2,8192]{5,4,1,3,2,0:T(2,128)(2,1)} %get-tuple-element.14) | data formatting | bytes 16777216 | tf_op jit(solution)/shard_map/reshape.56
  831.3 10.2 %fusion.14 = f32[128,2,32,64]{3,2,1,0:T(8,128)} fusion(bf16[2,128,32,512]{3,2,0,1:T(8,128)(2,1)} %reshape.563, bf16[2,128,64,512]{3,2,1,0:T(8,128)(2,1)} %param.9), kind=kOutput, calls=%fused_computation.31 | convolution fusion | flops 536870912 | bytes 18874368 | tf_op jit(solution)/shard_map/bnkum,kvm->bnkvu/dot_general | solution.py:39
  841.5 9.3 fusion.46
  854.1 10.2 %fusion.12 = f32[128,2,32,64]{3,2,1,0:T(8,128)} fusion(bf16[2,128,32,512]{3,2,0,1:T(8,128)(2,1)} %reshape.564, bf16[2,128,64,512]{3,2,1,0:T(8,128)(2,1)} %param.9), kind=kOutput, calls=%fused_computation.29 | convolution fusion | flops 536870912 | bytes 18874368 | tf_op jit(solution)/shard_map/bnkum,kvm->bnkvu/dot_general | solution.py:42
  864.3 10.7 %fusion.47 = bf16[2,1,128,64,32]{3,4,0,2,1:T(8,128)(2,1)} fusion(f32[128,2,32,64]{3,2,1,0:T(8,128)} %fusion.12, bf16[2,128,32,512]{3,2,0,1:T(8,128)(2,1)} %reshape.563, bf16[2,128,64,512]{3,2,1,0:T(8,128)(2,1)} %param.9), kind=kOutput, calls=%fused_computation.99 | convolution fusion | flops 537919488 | bytes 22020096 | tf_op jit(solution)/shard_map/bnkum,kvm->bnkvu/dot_general | solution.py:41
  875.0 4.5 copy.179
  896.2 4.5 collective-permute-start.6
  900.8 13.5 %collective-permute-done.4 = bf16[1,2,2,1,128,4,32]{4,6,5,0,3,2,1:T(8,128)(2,1)S(1)} collective-permute-done((bf16[1,2,2,1,128,4,32]{4,6,5,0,3,2,1:T(8,128)(2,1)S(1)}, bf16[1,2,2,1,128,4,32]{4,6,5,0,3,2,1:T(8,128)(2,1)S(1)}, u32[]{:S(2)}, u32[]{:S(2)}) %collective-permute-start.4) | collective-permute-done | bytes 131104 | tf_op jit(solution)/shard_map/ppermute | solution.py:27
  915.2 4.5 collective-permute-start.12
  939.1 7.0 fusion.5
  946.2 7.1 fusion.6
  953.2 7.0 fusion.4
  960.3 7.1 fusion.7
  971.1 12.3 %collective-permute-done.15 = bf16[2,2,1,128,4,128]{5,3,4,2,1,0:T(8,128)(2,1)S(1)} collective-permute-done((bf16[2,2,1,128,4,128]{5,3,4,2,1,0:T(8,128)(2,1)S(1)}, bf16[2,2,1,128,4,128]{5,3,4,2,1,0:T(8,128)(2,1)S(1)}, u32[]{:S(2)}, u32[]{:S(2)}) %collective-permute-start.15) | collective-permute-done | bytes 524320 | tf_op jit(solution)/shard_map/ppermute | solution.py:35
  (106 shorter events, 59.6 us)
Async XLA Ops:
  6.5 932.5 %all-gather.2.cloned.1.call-start = ((), (), s32[]{:S(2)}) async-start(), calls=%async_computation.2 | async-start | bytes 35651584 | tf_op jit(solution)/shard_map/all_gather | solution.py:110
  7.3 4.6 copy-start.3
  16.0 14.9 %slice-start = ((s8[16777216]{0:T(1024)(128)(4,1)}), s8[4194304]{0:T(1024)(128)(4,1)S(1)}, s32[]{:S(2)}) async-start(s8[16777216]{0:T(1024)(128)(4,1)} %bitcast.334), calls=%async_computation.3 | async-start | bytes 8388608
  16.0 14.9 %slice-start.1 = ((s8[16777216]{0:T(1024)(128)(4,1)}), s8[4194304]{0:T(1024)(128)(4,1)S(1)}, s32[]{:S(2)}) async-start(s8[16777216]{0:T(1024)(128)(4,1)} %bitcast.334), calls=%async_computation.4 | async-start | bytes 8388608
  20.0 10.9 %slice-start.2 = ((s8[16777216]{0:T(1024)(128)(4,1)}), s8[4194304]{0:T(1024)(128)(4,1)S(1)}, s32[]{:S(2)}) async-start(s8[16777216]{0:T(1024)(128)(4,1)} %bitcast.334), calls=%async_computation.5 | async-start | bytes 8388608
  25.5 5.4 slice-start.3
  54.8 16.5 %copy-start.4 = (bf16[2,128,64,32]{2,3,0,1:T(8,128)(2,1)S(1)}, bf16[2,128,64,32]{2,3,0,1:T(8,128)(2,1)}, u32[]{:S(2)}) copy-start(bf16[2,128,64,32]{2,3,0,1:T(8,128)(2,1)} %fusion.44) | copy-start | bytes 3145732
  71.3 12.1 %copy-start.2 = (bf16[2,128,64,32]{2,3,0,1:T(8,128)(2,1)S(1)}, bf16[2,128,64,32]{2,3,0,1:T(8,128)(2,1)}, u32[]{:S(2)}) copy-start(bf16[2,128,64,32]{2,3,0,1:T(8,128)(2,1)} %fusion.45) | copy-start | bytes 3145732
  138.4 192.7 %all-to-all-start = ((bf16[2,2,1,128,16384]{3,1,2,0,4:T(2,128)(2,1)}), bf16[2,2,1,128,16384]{3,1,2,0,4:T(2,128)(2,1)}, u32[]{:S(2)}, u32[]{:S(2)}) async-start(bf16[2,2,1,128,16384]{3,1,2,0,4:T(2,128)(2,1)} %pad_maximum_fusion), calls=%async_computation | async-start | bytes 33554432 | tf_op jit(solution)/shard_map/all_to_all | solution.py:78
  386.3 14.2 %copy-start.6 = (s32[256]{0:T(256)S(1)}, s32[256]{0:T(256)}, u32[]{:S(2)}) copy-start(s32[256]{0:T(256)} %param.14) | copy-start | bytes 3076
  400.5 12.6 %copy-start.1 = (bf16[2,256,8192]{1,2,0:T(8,128)(2,1)S(1)}, bf16[2,256,8192]{1,2,0:T(8,128)(2,1)}, u32[]{:S(2)}) copy-start(bf16[2,256,8192]{1,2,0:T(8,128)(2,1)} %reshape.559) | copy-start | bytes 25165828
  464.2 12.6 %copy-start = (bf16[2,256,8192]{1,2,0:T(8,128)(2,1)S(1)}, bf16[2,256,8192]{1,2,0:T(8,128)(2,1)}, u32[]{:S(2)}) copy-start(bf16[2,256,8192]{1,2,0:T(8,128)(2,1)} %get-tuple-element.12) | copy-start | bytes 25165828
  464.2 35.3 %slice-start.4 = ((s8[8388608]{0:T(1024)(128)(4,1)}), s8[4194304]{0:T(1024)(128)(4,1)S(1)}, s32[]{:S(2)}) async-start(s8[8388608]{0:T(1024)(128)(4,1)} %bitcast.336), calls=%async_computation.7 | async-start | bytes 8388608
  476.8 22.7 %slice-start.5 = ((s8[8388608]{0:T(1024)(128)(4,1)}), s8[4194304]{0:T(1024)(128)(4,1)S(1)}, s32[]{:S(2)}) async-start(s8[8388608]{0:T(1024)(128)(4,1)} %bitcast.336), calls=%async_computation.8 | async-start | bytes 8388608
  565.9 191.8 %all-to-all-start.1 = ((bf16[2,2,1,256,8192]{4,1,2,0,3:T(2,128)(2,1)}), bf16[2,2,1,256,8192]{4,1,2,0,3:T(2,128)(2,1)}, u32[]{:S(2)}, u32[]{:S(2)}) async-start(bf16[2,2,1,256,8192]{4,1,2,0,3:T(2,128)(2,1)} %copy.176), calls=%async_computation.1 | async-start | bytes 33554432 | tf_op jit(solution)/shard_map/all_to_all | solution.py:95
  879.5 50.7 %collective-permute-start.10 = (bf16[1,2,2,1,128,4,32]{4,6,5,0,3,2,1:T(8,128)(2,1)S(1)}, bf16[1,2,2,1,128,4,32]{4,6,5,0,3,2,1:T(8,128)(2,1)S(1)}, u32[]{:S(2)}, u32[]{:S(2)}) collective-permute-start(bf16[1,2,2,1,128,4,32]{4,6,5,0,3,2,1:T(8,128)(2,1)S(1)} %get-tuple-element.39), channel_id=1, source_target_pairs={{0,11},{1,12},{2,13},{3,14},{4,15},{5,0},{6,1},{7,2},{8,3},{9,4},{... | collective-permute-start | bytes 393224 | tf_op jit(solution)/shard_map/ppermute | solution.py:27
  880.7 8.5 collective-permute-start
  883.4 9.2 collective-permute-start.1
  884.4 29.9 %collective-permute-start.5 = (bf16[1,2,2,1,128,4,32]{4,6,5,0,3,2,1:T(8,128)(2,1)S(1)}, bf16[1,2,2,1,128,4,32]{4,6,5,0,3,2,1:T(8,128)(2,1)S(1)}, u32[]{:S(2)}, u32[]{:S(2)}) collective-permute-start(bf16[1,2,2,1,128,4,32]{4,6,5,0,3,2,1:T(8,128)(2,1)S(1)} %get-tuple-element.33), channel_id=1, source_target_pairs={{0,6},{1,7},{2,8},{3,9},{4,10},{5,11},{6,12},{7,13},{8,14},{9,15},... | collective-permute-start | bytes 393224 | tf_op jit(solution)/shard_map/ppermute | solution.py:27
  884.7 11.5 %collective-permute-start.2 = (bf16[1,2,2,1,128,4,32]{4,6,5,0,3,2,1:T(8,128)(2,1)S(1)}, bf16[1,2,2,1,128,4,32]{4,6,5,0,3,2,1:T(8,128)(2,1)S(1)}, u32[]{:S(2)}, u32[]{:S(2)}) collective-permute-start(bf16[1,2,2,1,128,4,32]{4,6,5,0,3,2,1:T(8,128)(2,1)S(1)} %get-tuple-element.29), channel_id=1, source_target_pairs={{0,3},{1,4},{2,5},{3,6},{4,7},{5,8},{6,9},{7,10},{8,11},{9,12},{10... | collective-permute-start | bytes 393224 | tf_op jit(solution)/shard_map/ppermute | solution.py:27
  889.1 11.6 %collective-permute-start.3 = (bf16[1,2,2,1,128,4,32]{4,6,5,0,3,2,1:T(8,128)(2,1)S(1)}, bf16[1,2,2,1,128,4,32]{4,6,5,0,3,2,1:T(8,128)(2,1)S(1)}, u32[]{:S(2)}, u32[]{:S(2)}) collective-permute-start(bf16[1,2,2,1,128,4,32]{4,6,5,0,3,2,1:T(8,128)(2,1)S(1)} %get-tuple-element.30), channel_id=1, source_target_pairs={{0,4},{1,5},{2,6},{3,7},{4,8},{5,9},{6,10},{7,11},{8,12},{9,13},{1... | collective-permute-start | bytes 393224 | tf_op jit(solution)/shard_map/ppermute | solution.py:27
  892.6 21.7 %collective-permute-start.4 = (bf16[1,2,2,1,128,4,32]{4,6,5,0,3,2,1:T(8,128)(2,1)S(1)}, bf16[1,2,2,1,128,4,32]{4,6,5,0,3,2,1:T(8,128)(2,1)S(1)}, u32[]{:S(2)}, u32[]{:S(2)}) collective-permute-start(bf16[1,2,2,1,128,4,32]{4,6,5,0,3,2,1:T(8,128)(2,1)S(1)} %get-tuple-element.31), channel_id=1, source_target_pairs={{0,5},{1,6},{2,7},{3,8},{4,9},{5,10},{6,11},{7,12},{8,13},{9,14},{... | collective-permute-start | bytes 393224 | tf_op jit(solution)/shard_map/ppermute | solution.py:27
  896.2 18.2 %collective-permute-start.6 = (bf16[1,2,2,1,128,4,32]{4,6,5,0,3,2,1:T(8,128)(2,1)S(1)}, bf16[1,2,2,1,128,4,32]{4,6,5,0,3,2,1:T(8,128)(2,1)S(1)}, u32[]{:S(2)}, u32[]{:S(2)}) collective-permute-start(bf16[1,2,2,1,128,4,32]{4,6,5,0,3,2,1:T(8,128)(2,1)S(1)} %get-tuple-element.34), channel_id=1, source_target_pairs={{0,7},{1,8},{2,9},{3,10},{4,11},{5,12},{6,13},{7,14},{8,15},{9,0},... | collective-permute-start | bytes 393224 | tf_op jit(solution)/shard_map/ppermute | solution.py:27
  900.7 14.5 %collective-permute-start.7 = (bf16[1,2,2,1,128,4,32]{4,6,5,0,3,2,1:T(8,128)(2,1)S(1)}, bf16[1,2,2,1,128,4,32]{4,6,5,0,3,2,1:T(8,128)(2,1)S(1)}, u32[]{:S(2)}, u32[]{:S(2)}) collective-permute-start(bf16[1,2,2,1,128,4,32]{4,6,5,0,3,2,1:T(8,128)(2,1)S(1)} %get-tuple-element.35), channel_id=1, source_target_pairs={{0,8},{1,9},{2,10},{3,11},{4,12},{5,13},{6,14},{7,15},{8,0},{9,1},... | collective-permute-start | bytes 393224 | tf_op jit(solution)/shard_map/ppermute | solution.py:27
  914.3 9.9 collective-permute-start.8
  914.3 13.8 %collective-permute-start.9 = (bf16[1,2,2,1,128,4,32]{4,6,5,0,3,2,1:T(8,128)(2,1)S(1)}, bf16[1,2,2,1,128,4,32]{4,6,5,0,3,2,1:T(8,128)(2,1)S(1)}, u32[]{:S(2)}, u32[]{:S(2)}) collective-permute-start(bf16[1,2,2,1,128,4,32]{4,6,5,0,3,2,1:T(8,128)(2,1)S(1)} %get-tuple-element.37), channel_id=1, source_target_pairs={{0,10},{1,11},{2,12},{3,13},{4,14},{5,15},{6,0},{7,1},{8,2},{9,3},... | collective-permute-start | bytes 393224 | tf_op jit(solution)/shard_map/ppermute | solution.py:27
  914.4 15.8 %collective-permute-start.11 = (bf16[1,2,2,1,128,4,32]{4,6,5,0,3,2,1:T(8,128)(2,1)S(1)}, bf16[1,2,2,1,128,4,32]{4,6,5,0,3,2,1:T(8,128)(2,1)S(1)}, u32[]{:S(2)}, u32[]{:S(2)}) collective-permute-start(bf16[1,2,2,1,128,4,32]{4,6,5,0,3,2,1:T(8,128)(2,1)S(1)} %get-tuple-element.40), channel_id=1, source_target_pairs={{0,12},{1,13},{2,14},{3,15},{4,0},{5,1},{6,2},{7,3},{8,4},{9,5},{1... | collective-permute-start | bytes 393224 | tf_op jit(solution)/shard_map/ppermute | solution.py:27
  915.2 15.1 %collective-permute-start.12 = (bf16[1,2,2,1,128,4,32]{4,6,5,0,3,2,1:T(8,128)(2,1)S(1)}, bf16[1,2,2,1,128,4,32]{4,6,5,0,3,2,1:T(8,128)(2,1)S(1)}, u32[]{:S(2)}, u32[]{:S(2)}) collective-permute-start(bf16[1,2,2,1,128,4,32]{4,6,5,0,3,2,1:T(8,128)(2,1)S(1)} %get-tuple-element.38), channel_id=1, source_target_pairs={{0,13},{1,14},{2,15},{3,0},{4,1},{5,2},{6,3},{7,4},{8,5},{9,6},{10... | collective-permute-start | bytes 393224 | tf_op jit(solution)/shard_map/ppermute | solution.py:27
  924.2 9.5 collective-permute-start.13
  928.2 6.0 collective-permute-start.14
  960.3 9.2 copy-start.8
  967.3 18.6 %copy-start.5 = (f32[128,128]{1,0:T(8,128)S(1)}, f32[128,128]{1,0:T(8,128)}, u32[]{:S(2)}) copy-start(f32[128,128]{1,0:T(8,128)} %param.13) | copy-start | bytes 196612
  967.4 18.6 %copy-start.7 = (f32[128,4]{0,1:T(4,128)S(1)}, f32[128,4]{0,1:T(4,128)}, u32[]{:S(2)}) copy-start(f32[128,4]{0,1:T(4,128)} %param.12) | copy-start | bytes 6148
  968.8 14.6 %collective-permute-start.15 = (bf16[2,2,1,128,4,128]{5,3,4,2,1,0:T(8,128)(2,1)S(1)}, bf16[2,2,1,128,4,128]{5,3,4,2,1,0:T(8,128)(2,1)S(1)}, u32[]{:S(2)}, u32[]{:S(2)}) collective-permute-start(bf16[2,2,1,128,4,128]{5,3,4,2,1,0:T(8,128)(2,1)S(1)} %pad_maximum_fusion.4), channel_id=1, source_target_pairs={{0,16},{16,0},{1,17},{17,1},{2,18},{18,2},{3,19},{19,3},{4,20},{20... | collective-permute-start | bytes 1572872 | tf_op jit(solution)/shard_map/ppermute | solution.py:35
Sparse Core Ops, SparseCore 0:
  8.9 170.7 all-gather.1
